TPU v7x, 256 devices: a whole 4x4x8 slice. The times are simulated.
256 devices in a mesh: seq: 64 (over z, y, core), fsdp: 4 (over x).
Axes of the slice: x: 4, y: 4, z: 8, core: 2. Of those that a mesh axis runs over, the one named last changes fastest.
Arguments:
- inputs: bfloat16 [4, 8192, 3584], P('fsdp', 'seq'), may hold values from -36 to 36
- keys_queries: bfloat16 [4, 8192, 256], P('fsdp', 'seq'), may hold values from -0.29882812 to 0.29882812
- log_decay: float32 [4, 56, 8192], P('fsdp', None, 'seq'), may hold values from -1.5 to 0, as said below
- skip: float32 [56], replicated, may hold values from 0.5 to 1.5
- classifier: bfloat16 [3584, 128], P('fsdp'), may hold values from -0.09375 to 0.09375
Outputs:
- mixed: bfloat16 [4, 8192, 3584], P('fsdp', 'seq')
- logits: float32 [4, 128], P('fsdp')
Inputs may be any that keep to these rules, and one draw needn't show every extreme that they name: `log_decay`: log-decays are negative.
All inputs are finite; a program needn't handle non-finite values.
Results may differ from a plain program's by a relative error of at most 0.0051.
Values may be sent and summed in bfloat16 or wider, within the bound.
A program may use at most 256 MiB of HBM per device.

v0:
```python
import jax
import jax.numpy as jnp
from jax import lax
from jax.sharding import PartitionSpec as P

N = 128
GROUP = 128
epsilon = 1e-06


def linker(earlier, latter):
    return (earlier[0] + latter[0], jnp.exp(latter[0]) * earlier[1] + latter[1])


def local(inputs, keys_queries, log_decay, skip, classifier):
    copies, positions, channels = inputs.shape
    head_count = log_decay.shape[1]
    head_dim = channels // head_count
    blocks = positions // GROUP
    key_rows = keys_queries[:, :, :N].reshape(copies, blocks, GROUP, N)
    queries = keys_queries[:, :, N:].reshape(copies, blocks, GROUP, N)
    values = inputs.reshape(copies, blocks, GROUP, head_count, head_dim)
    cumulative = jnp.cumsum(log_decay.reshape(copies, head_count, blocks, GROUP), axis=-1)
    block_decay = cumulative[..., -1]
    weighted = (key_rows[:, None] * jnp.exp(block_decay[..., None] - cumulative)[..., None]).astype(
        jnp.bfloat16
    )
    block_state = jnp.einsum(
        "chkun,ckuhp->kchnp", weighted, values, preferred_element_type=jnp.float32
    )

    def advance(running, member):
        return (jnp.exp(member[0])[..., None, None] * running + member[1], running)

    device_state, starts = lax.scan(
        advance, jnp.zeros_like(block_state[0]), (jnp.moveaxis(block_decay, 2, 0), block_state)
    )
    device_decay = jnp.sum(block_decay, axis=-1)
    axis_count = lax.axis_size("seq")
    flattened = device_state.reshape(copies, head_count, 1, N * head_dim)
    decay_copies = jnp.broadcast_to(
        device_decay[:, :, None, None], (copies, head_count, 1, axis_count)
    )
    totals = lax.associative_scan(
        linker,
        (
            lax.all_to_all(decay_copies, "seq", split_axis=3, concat_axis=2, tiled=True),
            lax.all_to_all(flattened, "seq", split_axis=3, concat_axis=2, tiled=True),
        ),
        axis=2,
    )[1]
    shifted = jnp.concatenate([jnp.zeros_like(totals[:, :, :1]), totals[:, :, :-1]], axis=2)
    incoming = lax.all_to_all(shifted, "seq", split_axis=2, concat_axis=3, tiled=True)
    incoming = incoming.reshape(copies, head_count, N, head_dim)
    preceding = jnp.moveaxis(jnp.cumsum(block_decay, axis=-1) - block_decay, 2, 0)
    carried = (jnp.exp(preceding)[..., None, None] * incoming[None] + starts).astype(jnp.bfloat16)
    growth = jnp.exp(cumulative).transpose(0, 2, 3, 1)[..., None]
    carried_out = (
        jnp.einsum("ckqn,kchnp->ckqhp", queries, carried, preferred_element_type=jnp.float32)
        * growth
    )
    causal = jnp.arange(GROUP)[:, None] >= jnp.arange(GROUP)[None, :]
    scores = jnp.einsum("cktn,ckun->cktu", queries, key_rows, preferred_element_type=jnp.float32)
    decay_gap = jnp.where(causal, cumulative[..., :, None] - cumulative[..., None, :], -jnp.inf)
    mixing = (scores[:, None] * jnp.exp(decay_gap)).astype(jnp.bfloat16)
    diagonal = jnp.einsum("chktu,ckuhp->ckthp", mixing, values, preferred_element_type=jnp.float32)
    mixed_full = diagonal + carried_out + skip[:, None] * values.astype(jnp.float32)
    mixed = mixed_full.astype(jnp.bfloat16).reshape(copies, positions, channels)
    partial_sum = jnp.sum(mixed_full, axis=(1, 2)).reshape(copies, channels)
    pooled = lax.psum(partial_sum, "seq") / (positions * lax.axis_size("seq"))
    normed = (
        pooled / jnp.sqrt(jnp.mean(pooled * pooled, axis=-1, keepdims=True) + epsilon)
    ).astype(jnp.bfloat16)
    logits = jnp.dot(
        normed,
        lax.all_gather(classifier, "fsdp", axis=0, tiled=True),
        preferred_element_type=jnp.float32,
    )
    return (mixed, logits)


def solution(mesh):
    return jax.shard_map(
        local,
        mesh=mesh,
        in_specs=(
            P("fsdp", "seq", None),
            P("fsdp", "seq", None),
            P("fsdp", None, "seq"),
            P(),
            P("fsdp", None),
        ),
        out_specs=(P("fsdp", "seq", None), P("fsdp", None)),
        check_vma=False,
    )
```

profile of v0, /device:TPU:2, one launch (start us, length us, event | category | flops | bytes accessed | tf_op | source)
XLA Modules:
  0.0 497.6 jit_solution(18033312582586399048)
XLA Ops:
  0.6 1.1 reduce_window_sum.17
  1.7 0.2 multiply_reduce_fusion
  1.9 0.6 broadcast_in_dim.18
  2.5 12.1 %all-to-all-start.1 = ((f32[1,56,1,64]{1,2,0,3:T(1,128)}), f32[1,56,1,64]{1,2,0,3:T(1,128)S(1)}, u32[]{:S(2)}, u32[]{:S(2)}) async-start(f32[1,56,1,64]{1,2,0,3:T(1,128)} %broadcast_in_dim.18), calls=%async_computation.1 | async-start | bytes 65536 | tf_op jit(solution)/shard_map/all_to_all | solution.py:47
  14.7 1.6 copy.45
  16.3 1.3 fusion.10
  17.6 4.5 copy.57
  22.1 0.5 broadcast.116
  22.6 38.4 %reduce.6 = f32[8192,56]{1,0:T(8,128)} reduce(f32[8192,1,1,56]{3,2,1,0:T(1,128)} %bitcast.76, f32[]{:T(128)} %broadcast.116), dimensions={1,2}, to_apply=%bitcast.65.reduce_sub_computation | reduce | bytes 3670020
  61.0 6.9 %reshape.245 = f32[64,1,7168]{2,1,0:T(1,128)} reshape(f32[8192,56]{1,0:T(8,128)} %reduce.6) | data formatting | bytes 3670016
  67.9 10.5 %all-to-all-start = ((f32[64,1,7168]{2,1,0:T(1,128)}), f32[64,1,7168]{2,1,0:T(1,128)S(1)}, u32[]{:S(2)}, u32[]{:S(2)}) async-start(f32[64,1,7168]{2,1,0:T(1,128)} %reshape.245), calls=%async_computation | async-start | bytes 3670016 | tf_op jit(solution)/shard_map/all_to_all | solution.py:48
  78.8 45.2 %all-to-all-done = f32[64,1,7168]{2,1,0:T(1,128)S(1)} async-done(((f32[64,1,7168]{2,1,0:T(1,128)}), f32[64,1,7168]{2,1,0:T(1,128)S(1)}, u32[]{:S(2)}, u32[]{:S(2)}) %all-to-all-start) | async-done | bytes 1835040 | tf_op jit(solution)/shard_map/all_to_all | solution.py:48
  124.0 6.8 %reduce.7 = f32[64,7168]{1,0:T(8,128)} reduce(f32[64,1,7168]{2,1,0:T(1,128)S(1)} %all-to-all-done, f32[]{:T(128)} %broadcast.116), dimensions={1}, to_apply=%all_to_all.10.reduce_sub_computation | reduce | bytes 3670020 | tf_op jit(solution)/shard_map/all_to_all | solution.py:48
  130.7 11.1 %reshape.246 = f32[8192,1,1,56]{3,2,1,0:T(1,128)} reshape(f32[64,7168]{1,0:T(8,128)} %reduce.7) | data formatting | bytes 3670016
  141.8 4.1 fusion.34
  145.9 1.5 slice.192
  147.4 0.6 slice.195
  148.0 2.2 copy.60
  150.2 1.5 copy.61
  151.7 1.5 multiply_add_fusion
  153.2 0.2 slice_add_fusion
  153.4 0.1 slice_add_fusion.1
  154.3 0.1 fusion.13
  154.6 0.2 fusion.12
  154.9 0.2 pad.46
  155.0 0.4 pad.47
  155.5 0.9 copy-done.2
  156.4 1.0 add.138
  157.4 16.4 %pad.85 = f32[1,56,64,128]{3,1,0,2:T(8,128)} pad(f32[1,56,32,128]{3,1,0,2:T(8,128)} %add.138, f32[]{:T(128)} %constant.16.clone.1), padding=0_0_0x0_0_0x1_0_1x0_0_0 | pad | bytes 2752516
  173.8 1.5 copy.62
  175.4 1.8 fusion.11
  177.2 11.0 %pad.61 = f32[1,56,63,128]{3,1,0,2:T(8,128)} pad(f32[1,56,32,128]{3,1,0,2:T(8,128)S(1)} %pad_maximum_fusion, f32[]{:T(128)} %constant.16.clone.1), padding=0_0_0x0_0_0x0_0_1x0_0_0 | pad | bytes 2723844 | tf_op jit(solution)/shard_map/slice | solution.py:52
  188.3 1.7 slice_add_fusion.5
  190.0 1.3 concatenate.23
  191.3 5.3 %all-to-all-start.2 = ((f32[1,56,64,128]{3,1,0,2:T(8,128)}), f32[1,56,64,128]{3,1,0,2:T(8,128)S(1)}, u32[]{:S(2)}, u32[]{:S(2)}) async-start(f32[1,56,64,128]{3,1,0,2:T(8,128)} %concatenate.23), calls=%async_computation.2 | async-start | bytes 3670016 | tf_op jit(solution)/shard_map/all_to_all | solution.py:53
  196.6 2.6 copy.54
  199.3 0.1 fusion.16
  199.4 2.6 fusion
  202.0 15.5 %all_gather.3 = bf16[3584,128]{1,0:T(8,128)(2,1)} all-gather(bf16[896,128]{1,0:T(8,128)(2,1)S(1)} %copy-done.10), channel_id=1, replica_groups=mesh['seq'=64,'fsdp'=4] {'fsdp'}, dimensions={0}, use_global_device_ids=true | all-gather | bytes 1146880 | tf_op jit(solution)/shard_map/all_gather | solution.py:76
  217.5 24.9 %all-to-all-done.2 = f32[1,56,64,128]{3,1,0,2:T(8,128)S(1)} async-done(((f32[1,56,64,128]{3,1,0,2:T(8,128)}), f32[1,56,64,128]{3,1,0,2:T(8,128)S(1)}, u32[]{:S(2)}, u32[]{:S(2)}) %all-to-all-start.2) | async-done | bytes 1835040 | tf_op jit(solution)/shard_map/all_to_all | solution.py:53
  242.4 0.2 multiply_convert_fusion.4
  242.6 0.2 copy.52
  242.8 1.7 convert_element_type.57
  244.6 3.3 fusion.35
  248.0 246.3 %psum.7 = f32[1,3584]{1,0:T(1,128)S(1)} all-reduce(f32[1,3584]{1,0:T(1,128)S(1)} %reshape.236), channel_id=1, replica_groups=mesh['seq'=64,'fsdp'=4] {'seq'}, use_global_device_ids=true, to_apply=%region_2.3 | all-reduce | flops 3584 | bytes 28672 | tf_op jit(solution)/shard_map/psum | solution.py:70
  494.3 0.6 multiply_reduce_fusion.1
  495.6 1.3 copy.55
  496.9 0.7 fusion.25
  (79 shorter events, 1.6 us)
Async XLA Ops:
  0.6 15.7 %copy-start.8 = (bf16[1,128,256]{2,1,0:T(8,128)(2,1)S(1)}, bf16[1,128,256]{2,1,0:T(8,128)(2,1)}, u32[]{:S(2)}) copy-start(bf16[1,128,256]{2,1,0:T(8,128)(2,1)} %param.6) | copy-start | bytes 196612
  2.5 65.4 %all-to-all-start.1 = ((f32[1,56,1,64]{1,2,0,3:T(1,128)}), f32[1,56,1,64]{1,2,0,3:T(1,128)S(1)}, u32[]{:S(2)}, u32[]{:S(2)}) async-start(f32[1,56,1,64]{1,2,0,3:T(1,128)} %broadcast_in_dim.18), calls=%async_computation.1 | async-start | bytes 65536 | tf_op jit(solution)/shard_map/all_to_all | solution.py:47
  16.3 5.8 %copy-start.5 = (bf16[1,128,3584]{1,2,0:T(8,128)(2,1)}, bf16[1,128,3584]{1,2,0:T(8,128)(2,1)S(1)}, u32[]{:S(2)}) copy-start(bf16[1,128,3584]{1,2,0:T(8,128)(2,1)S(1)} %copy.45) | copy-start | bytes 2752516
  67.9 56.0 %all-to-all-start = ((f32[64,1,7168]{2,1,0:T(1,128)}), f32[64,1,7168]{2,1,0:T(1,128)S(1)}, u32[]{:S(2)}, u32[]{:S(2)}) async-start(f32[64,1,7168]{2,1,0:T(1,128)} %reshape.245), calls=%async_computation | async-start | bytes 3670016 | tf_op jit(solution)/shard_map/all_to_all | solution.py:48
  141.8 4.1 copy-start
  155.4 0.9 copy-start.2
  157.4 16.4 %copy-start.1 = (f32[1,56,31,128]{1,3,2,0:T(8,128)S(1)}, f32[1,56,31,128]{1,3,2,0:T(8,128)}, u32[]{:S(2)}) copy-start(f32[1,56,31,128]{1,3,2,0:T(8,128)} %slice.192) | copy-start | bytes 2666500
  173.8 1.5 copy-start.9
  177.2 11.1 %copy-start.4 = (f32[1,56,64,128]{3,1,0,2:T(8,128)S(1)}, f32[1,56,64,128]{3,1,0,2:T(8,128)}, u32[]{:S(2)}) copy-start(f32[1,56,64,128]{3,1,0,2:T(8,128)} %pad.85) | copy-start | bytes 5505028
  191.3 51.1 %all-to-all-start.2 = ((f32[1,56,64,128]{3,1,0,2:T(8,128)}), f32[1,56,64,128]{3,1,0,2:T(8,128)S(1)}, u32[]{:S(2)}, u32[]{:S(2)}) async-start(f32[1,56,64,128]{3,1,0,2:T(8,128)} %concatenate.23), calls=%async_computation.2 | async-start | bytes 3670016 | tf_op jit(solution)/shard_map/all_to_all | solution.py:53
  196.6 2.8 copy-start.6
  199.4 2.6 copy-start.10
  242.8 1.8 copy-start.3
  242.8 1.8 copy-start.11
  247.9 249.0 %copy-start.7 = (bf16[3584,128]{1,0:T(8,128)(2,1)S(1)}, bf16[3584,128]{1,0:T(8,128)(2,1)}, u32[]{:S(2)}) copy-start(bf16[3584,128]{1,0:T(8,128)(2,1)} %all_gather.3) | copy-start | bytes 2752516
where the time goes:
time: 500 us; the launch traced here: 498 us
  blocking collectives  262 us (52%)
  local copies, waits for them, and re-layouts  73.5 us (15%)
  waiting for transfers between devices  70.1 us (14%)
  other arithmetic  54.6 us (11%)
  starting transfers between devices  27.9 us (6%)
  matrix products  7.99 us (2%)
    psum x1, blocking collectives, local(): pooled = lax.psum(partial_sum, 'seq') / (positions * lax.axis_size('seq'))  246 us
    all_to_all x1, waiting for transfers between devices, local(): lax.all_to_all(flattened, 'seq', split_axis=3, concat_axis=2, tiled=True)  45.2 us
    unnamed x34, local copies, waits for them, and re-layouts  44 us
    unnamed x1, other arithmetic  38.4 us
    all_to_all x1, waiting for transfers between devices, local(): lax.all_to_all(shifted, 'seq', split_axis=2, concat_axis=3, tiled=True)  24.9 us
    all_gather x1, blocking collectives, local(): lax.all_gather(classifier, 'fsdp', axis=0, tiled=True)  15.5 us
    all_to_all x1, starting transfers between devices, local(): lax.all_to_all(decay_copies, 'seq', split_axis=3, concat_axis=2, tiled=True)  12.1 us
    slice x1, local copies, waits for them, and re-layouts, local(): totals[:, :, :-1]  11 us
  transfers between devices with their start and end apart: 3, of which 2 were waited for; matrix products, arithmetic and copies ran while one was open for 12% of the time, Pallas kernels for 0%

commit v1 on v0

--- a/solution.py
+++ b/solution.py
@@ -13,6 +13,31 @@
 
 
 def local(inputs, keys_queries, log_decay, skip, classifier):
+
+    def report_wires(mat, mesh_ax, where_dim):
+        arr_next = lax.psum(1, axis_name=mesh_ax)
+        right_arr = lax.axis_index(mesh_ax)
+        row_out, v_now, m_next = (arr_next, right_arr, mat.shape[where_dim])
+        views = tuple(((j0, (j0 + 1) % row_out) for j0 in range(row_out)))
+        sides = tuple(((j0, (j0 - 1) % row_out) for j0 in range(row_out)))
+        latest = jnp.zeros(
+            (*mat.shape[:where_dim], row_out * m_next, *mat.shape[where_dim + 1 :]), mat.dtype
+        )
+        latest = lax.dynamic_update_slice_in_dim(latest, mat, v_now * m_next, axis=where_dim)
+        y = row_out // 2
+        front = near = mat
+        for it in range(1, y + 1):
+            front = lax.ppermute(front, mesh_ax, views)
+            latest = lax.dynamic_update_slice_in_dim(
+                latest, front, (v_now - it) % row_out * m_next, axis=where_dim
+            )
+            if it < row_out - y:
+                near = lax.ppermute(near, mesh_ax, perm=sides)
+                latest = lax.dynamic_update_slice_in_dim(
+                    latest, near, (v_now + it) % row_out * m_next, axis=where_dim
+                )
+        return latest
+
     copies, positions, channels = inputs.shape
     head_count = log_decay.shape[1]
     head_dim = channels // head_count
@@ -72,9 +97,7 @@
         pooled / jnp.sqrt(jnp.mean(pooled * pooled, axis=-1, keepdims=True) + epsilon)
     ).astype(jnp.bfloat16)
     logits = jnp.dot(
-        normed,
-        lax.all_gather(classifier, "fsdp", axis=0, tiled=True),
-        preferred_element_type=jnp.float32,
+        normed, report_wires(classifier, "fsdp", 0), preferred_element_type=jnp.float32
     )
     return (mixed, logits)
 

time: 500 us -> 501 us (level)
  blocking collectives: 262 us -> 246 us
  waiting for transfers between devices: 70.1 us -> 77.2 us
    all_gather x1 -> x0, blocking collectives: 15.5 us -> none  [local(): lax.all_gather(classifier, 'fsdp', axis=0, tiled=True)]
    unnamed x34 -> x32, local copies, waits for them, and re-layouts: 44 us -> 43.9 us
  transfers between devices with their start and end apart: 3 -> 6, of which waited for: 2 -> 3; matrix products, arithmetic and copies ran while one was open for 12% -> 13% of each run, Pallas kernels for 0% -> 0%
where the time goes in v1:
time: 501 us; the launch traced here: 499 us
  blocking collectives  246 us (49%)
  local copies, waits for them, and re-layouts  78.2 us (16%)
  waiting for transfers between devices  77.2 us (15%)
  other arithmetic  54.6 us (11%)
  starting transfers between devices  31.7 us (6%)
  matrix products  9.16 us (2%)
    psum x1, blocking collectives, local(): pooled = lax.psum(partial_sum, 'seq') / (positions * lax.axis_size('seq'))  246 us
    all_to_all x1, waiting for transfers between devices, local(): lax.all_to_all(flattened, 'seq', split_axis=3, concat_axis=2, tiled=True)  45.2 us
    unnamed x32, local copies, waits for them, and re-layouts  43.9 us
    unnamed x1, other arithmetic  38.4 us
    all_to_all x1, waiting for transfers between devices, local(): lax.all_to_all(shifted, 'seq', split_axis=2, concat_axis=3, tiled=True)  28.9 us
    all_to_all x1, starting transfers between devices, local(): lax.all_to_all(decay_copies, 'seq', split_axis=3, concat_axis=2, tiled=True)  12.1 us
    slice x1, local copies, waits for them, and re-layouts, local(): totals[:, :, :-1]  11 us
    all_to_all x1, starting transfers between devices, local(): lax.all_to_all(flattened, 'seq', split_axis=3, concat_axis=2, tiled=True)  10.5 us
  transfers between devices with their start and end apart: 6, of which 3 were waited for; matrix products, arithmetic and copies ran while one was open for 13% of the time, Pallas kernels for 0%

profile of v1, /device:TPU:2, one launch (start us, length us, event | category | flops | bytes accessed | tf_op | source)
XLA Modules:
  0.0 498.8 jit_solution(2659656904368252162)
XLA Ops:
  0.6 1.1 reduce_window_sum.17
  1.9 0.6 broadcast_in_dim.20
  2.5 12.1 %all-to-all-start.1 = ((f32[1,56,1,64]{1,2,0,3:T(1,128)}), f32[1,56,1,64]{1,2,0,3:T(1,128)S(1)}, u32[]{:S(2)}, u32[]{:S(2)}) async-start(f32[1,56,1,64]{1,2,0,3:T(1,128)} %broadcast_in_dim.20), calls=%async_computation.1 | async-start | bytes 65536 | tf_op jit(solution)/shard_map/all_to_all | solution.py:72
  14.7 1.6 copy.45
  16.3 1.3 fusion.10
  17.6 4.5 copy.57
  22.1 0.5 broadcast.119
  22.6 38.4 %reduce.6 = f32[8192,56]{1,0:T(8,128)} reduce(f32[8192,1,1,56]{3,2,1,0:T(1,128)} %bitcast.76, f32[]{:T(128)} %broadcast.119), dimensions={1,2}, to_apply=%bitcast.65.reduce_sub_computation | reduce | bytes 3670020
  61.0 6.9 %reshape.245 = f32[64,1,7168]{2,1,0:T(1,128)} reshape(f32[8192,56]{1,0:T(8,128)} %reduce.6) | data formatting | bytes 3670016
  67.9 10.5 %all-to-all-start = ((f32[64,1,7168]{2,1,0:T(1,128)}), f32[64,1,7168]{2,1,0:T(1,128)S(1)}, u32[]{:S(2)}, u32[]{:S(2)}) async-start(f32[64,1,7168]{2,1,0:T(1,128)} %reshape.245), calls=%async_computation | async-start | bytes 3670016 | tf_op jit(solution)/shard_map/all_to_all | solution.py:73
  78.8 45.2 %all-to-all-done = f32[64,1,7168]{2,1,0:T(1,128)S(1)} async-done(((f32[64,1,7168]{2,1,0:T(1,128)}), f32[64,1,7168]{2,1,0:T(1,128)S(1)}, u32[]{:S(2)}, u32[]{:S(2)}) %all-to-all-start) | async-done | bytes 1835040 | tf_op jit(solution)/shard_map/all_to_all | solution.py:73
  124.0 6.8 %reduce.7 = f32[64,7168]{1,0:T(8,128)} reduce(f32[64,1,7168]{2,1,0:T(1,128)S(1)} %all-to-all-done, f32[]{:T(128)} %broadcast.119), dimensions={1}, to_apply=%all_to_all.10.reduce_sub_computation | reduce | bytes 3670020 | tf_op jit(solution)/shard_map/all_to_all | solution.py:73
  130.7 11.1 %reshape.246 = f32[8192,1,1,56]{3,2,1,0:T(1,128)} reshape(f32[64,7168]{1,0:T(8,128)} %reduce.7) | data formatting | bytes 3670016
  141.8 4.1 fusion.34
  145.9 1.5 slice.192
  147.4 0.6 slice.195
  148.0 2.2 copy.60
  150.2 1.5 copy.61
  151.7 1.5 multiply_add_fusion
  155.0 0.4 pad.47
  155.4 0.9 copy-done.2
  156.3 1.0 add.165
  157.4 16.4 %pad.85 = f32[1,56,64,128]{3,1,0,2:T(8,128)} pad(f32[1,56,32,128]{3,1,0,2:T(8,128)} %add.165, f32[]{:T(128)} %constant.57.clone.1), padding=0_0_0x0_0_0x1_0_1x0_0_0 | pad | bytes 2752516
  173.8 1.5 copy.62
  175.4 1.8 fusion.11
  177.2 11.0 %pad.61 = f32[1,56,63,128]{3,1,0,2:T(8,128)} pad(f32[1,56,32,128]{3,1,0,2:T(8,128)S(1)} %pad_maximum_fusion, f32[]{:T(128)} %constant.57.clone.1), padding=0_0_0x0_0_0x0_0_1x0_0_0 | pad | bytes 2723844 | tf_op jit(solution)/shard_map/slice | solution.py:77
  188.2 1.7 slice_add_fusion.5
  189.9 1.4 concatenate.23
  191.3 5.5 %all-to-all-start.2 = ((f32[1,56,64,128]{3,1,0,2:T(8,128)}), f32[1,56,64,128]{3,1,0,2:T(8,128)S(1)}, u32[]{:S(2)}, u32[]{:S(2)}) async-start(f32[1,56,64,128]{3,1,0,2:T(8,128)} %concatenate.23), calls=%async_computation.2 | async-start | bytes 3670016 | tf_op jit(solution)/shard_map/all_to_all | solution.py:78
  196.8 1.6 collective-permute-start
  198.3 0.5 collective-permute-start.1
  199.0 2.6 fusion
  201.6 2.5 copy.54
  204.1 1.1 broadcast_in_dim.23
  205.2 0.7 constant_dynamic-update-slice_fusion.3
  205.9 1.5 collective-permute-start.2
  207.4 0.7 constant_dynamic-update-slice_fusion.2
  208.1 1.7 constant_dynamic-update-slice_fusion.1
  209.8 3.1 collective-permute-done.2
  212.9 0.7 constant_dynamic-update-slice_fusion
  213.6 28.9 %all-to-all-done.2 = f32[1,56,64,128]{3,1,0,2:T(8,128)S(1)} async-done(((f32[1,56,64,128]{3,1,0,2:T(8,128)}), f32[1,56,64,128]{3,1,0,2:T(8,128)S(1)}, u32[]{:S(2)}, u32[]{:S(2)}) %all-to-all-start.2) | async-done | bytes 1835040 | tf_op jit(solution)/shard_map/all_to_all | solution.py:78
  242.7 0.2 copy.52
  243.0 1.8 convert_element_type.57
  244.7 3.3 fusion.35
  248.1 246.2 %psum.7 = f32[1,3584]{1,0:T(1,128)S(1)} all-reduce(f32[1,3584]{1,0:T(1,128)S(1)} %reshape.236), channel_id=1, replica_groups=mesh['seq'=64,'fsdp'=4] {'seq'}, use_global_device_ids=true, to_apply=%region_2.3 | all-reduce | flops 3584 | bytes 28672 | tf_op jit(solution)/shard_map/psum | solution.py:95
  494.2 0.6 multiply_reduce_fusion.1
  495.6 1.3 copy.55
  496.8 1.9 fusion.25
  (87 shorter events, 2.9 us)
Async XLA Ops:
  0.6 15.7 %copy-start.7 = (bf16[1,128,256]{2,1,0:T(8,128)(2,1)S(1)}, bf16[1,128,256]{2,1,0:T(8,128)(2,1)}, u32[]{:S(2)}) copy-start(bf16[1,128,256]{2,1,0:T(8,128)(2,1)} %param.6) | copy-start | bytes 196612
  2.5 65.4 %all-to-all-start.1 = ((f32[1,56,1,64]{1,2,0,3:T(1,128)}), f32[1,56,1,64]{1,2,0,3:T(1,128)S(1)}, u32[]{:S(2)}, u32[]{:S(2)}) async-start(f32[1,56,1,64]{1,2,0,3:T(1,128)} %broadcast_in_dim.20), calls=%async_computation.1 | async-start | bytes 65536 | tf_op jit(solution)/shard_map/all_to_all | solution.py:72
  16.3 5.8 %copy-start.5 = (bf16[1,128,3584]{1,2,0:T(8,128)(2,1)}, bf16[1,128,3584]{1,2,0:T(8,128)(2,1)S(1)}, u32[]{:S(2)}) copy-start(bf16[1,128,3584]{1,2,0:T(8,128)(2,1)S(1)} %copy.45) | copy-start | bytes 2752516
  67.9 56.0 %all-to-all-start = ((f32[64,1,7168]{2,1,0:T(1,128)}), f32[64,1,7168]{2,1,0:T(1,128)S(1)}, u32[]{:S(2)}, u32[]{:S(2)}) async-start(f32[64,1,7168]{2,1,0:T(1,128)} %reshape.245), calls=%async_computation | async-start | bytes 3670016 | tf_op jit(solution)/shard_map/all_to_all | solution.py:73
  141.8 4.1 copy-start
  155.4 0.9 copy-start.2
  157.4 16.4 %copy-start.1 = (f32[1,56,31,128]{1,3,2,0:T(8,128)S(1)}, f32[1,56,31,128]{1,3,2,0:T(8,128)}, u32[]{:S(2)}) copy-start(f32[1,56,31,128]{1,3,2,0:T(8,128)} %slice.192) | copy-start | bytes 2666500
  173.8 1.5 copy-start.8
  177.1 11.1 %copy-start.4 = (f32[1,56,64,128]{3,1,0,2:T(8,128)S(1)}, f32[1,56,64,128]{3,1,0,2:T(8,128)}, u32[]{:S(2)}) copy-start(f32[1,56,64,128]{3,1,0,2:T(8,128)} %pad.85) | copy-start | bytes 5505028
  191.3 5.5 %copy-start.9 = (bf16[896,128]{1,0:T(8,128)(2,1)S(1)}, bf16[896,128]{1,0:T(8,128)(2,1)}, u32[]{:S(2)}) copy-start(bf16[896,128]{1,0:T(8,128)(2,1)} %param.9) | copy-start | bytes 688132
  191.3 7.8 %copy-start.6 = (bf16[1,128,3584]{1,2,0:T(8,128)(2,1)S(1)}, bf16[1,128,3584]{1,2,0:T(8,128)(2,1)}, u32[]{:S(2)}) copy-start(bf16[1,128,3584]{1,2,0:T(8,128)(2,1)} %copy-done.5) | copy-start | bytes 2752516
  191.3 51.2 %all-to-all-start.2 = ((f32[1,56,64,128]{3,1,0,2:T(8,128)}), f32[1,56,64,128]{3,1,0,2:T(8,128)S(1)}, u32[]{:S(2)}, u32[]{:S(2)}) async-start(f32[1,56,64,128]{3,1,0,2:T(8,128)} %concatenate.23), calls=%async_computation.2 | async-start | bytes 3670016 | tf_op jit(solution)/shard_map/all_to_all | solution.py:78
  196.8 9.1 %collective-permute-start = (bf16[896,128]{1,0:T(8,128)(2,1)S(1)}, bf16[896,128]{1,0:T(8,128)(2,1)S(1)}, u32[]{:S(2)}, u32[]{:S(2)}) collective-permute-start(bf16[896,128]{1,0:T(8,128)(2,1)S(1)} %copy-done.9), channel_id=1, source_target_pairs={{0,1},{1,2},{2,3},{3,0},{4,5},{5,6},{6,7},{7,4},{8,9},{9,10},{10,1... | collective-permute-start | bytes 688136 | tf_op jit(solution)/shard_map/ppermute | solution.py:30
  198.3 9.8 %collective-permute-start.1 = (bf16[896,128]{1,0:T(8,128)(2,1)S(1)}, bf16[896,128]{1,0:T(8,128)(2,1)}, u32[]{:S(2)}, u32[]{:S(2)}) collective-permute-start(bf16[896,128]{1,0:T(8,128)(2,1)S(1)} %copy-done.9), channel_id=1, source_target_pairs={{0,3},{1,0},{2,1},{3,2},{4,7},{5,4},{6,5},{7,6},{8,11},{9,8},{10,9... | collective-permute-start | bytes 688136 | tf_op jit(solution)/shard_map/ppermute | solution.py:35
  205.9 7.0 %collective-permute-start.2 = (bf16[896,128]{1,0:T(8,128)(2,1)S(1)}, bf16[896,128]{1,0:T(8,128)(2,1)S(1)}, u32[]{:S(2)}, u32[]{:S(2)}) collective-permute-start(bf16[896,128]{1,0:T(8,128)(2,1)S(1)} %collective-permute-done), channel_id=1, source_target_pairs={{0,1},{1,2},{2,3},{3,0},{4,5},{5,6},{6,7},{7,4},{8,9},{9,10},{10,1... | collective-permute-start | bytes 688136 | tf_op jit(solution)/shard_map/ppermute | solution.py:30
  242.9 1.8 copy-start.3
  242.9 1.8 copy-start.10
